TPU v7x, 32 devices: a whole 2x2x4 slice. The times are simulated.
32 devices in a mesh: gx: 4 (over y, core), gy: 8 (over z, x).
Axes of the slice: x: 2, y: 2, z: 4, core: 2. Of those that a mesh axis runs over, the one named last changes fastest.
Arguments:
- perturbation: float32 [5, 16, 512], P(None, 'gx', 'gy'), may hold values from -6 to 6
- mean_velocity: float32 [16, 512], P('gx', 'gy'), may hold values from 0.2 to 0.9
- mean_shear: float32 [16, 512], P('gx', 'gy'), may hold values from -4 to 4
- cotangent: float32 [5, 16, 512], P(None, 'gx', 'gy'), may hold values from -6 to 6
- kernel_in: bfloat16 [64, 135], replicated, may hold values from -0.5 to 0.5
- kernel_mid: bfloat16 [64, 1728], replicated, may hold values from -0.15625 to 0.15625
- kernel_out: bfloat16 [5, 1728], replicated, may hold values from -0.15625 to 0.15625
Outputs:
- advanced: float32 [5, 16, 512], P(None, 'gx', 'gy')
- grad_in: float32 [64, 135], replicated
- grad_mid: float32 [64, 1728], replicated
- grad_out: float32 [5, 1728], replicated
All inputs are finite; a program needn't handle non-finite values.
Results may differ from a plain program's by a relative error of at most 0.0065.
Values may be sent and summed in bfloat16 or wider, within the bound.
A program may use at most 64 MiB of HBM per device.

v0:
```python
import math
import jax
import jax.numpy as jnp
from jax import lax
from jax.sharding import PartitionSpec as P

NZ = 8
STEPS = 2
TIME_STEP = 0.25
STENCIL_WEIGHTS = (0.75, -0.15, 1.0 / 60.0)


def padded_2(cells, sides, width):
    for axis, dim in sides:
        count = lax.axis_size(axis)
        ends = count - 1
        head = lax.slice_in_dim(cells, 0, width, axis=dim)
        tail = lax.slice_in_dim(cells, cells.shape[dim] - width, cells.shape[dim], axis=dim)
        cells = jnp.concatenate(
            [
                lax.ppermute(tail, axis, [(i, (i + 1) % count) for i in range(ends)]),
                cells,
                lax.ppermute(head, axis, [((i + 1) % count, i) for i in range(ends)]),
            ],
            axis=dim,
        )
    return cells


def wrap_depth(grid_field, margin):
    size_z = grid_field.shape[3]
    return jnp.concatenate(
        [grid_field[:, :, :, size_z - margin :], grid_field, grid_field[:, :, :, :margin]], axis=3
    )


def difference(padded, direction, margin, length):
    summed = None
    for offset, weight in zip((1, 2, 3), STENCIL_WEIGHTS):
        upper_cells = lax.slice_in_dim(
            padded, margin + offset, margin + offset + length, axis=direction
        )
        lower_cells = lax.slice_in_dim(
            padded, margin - offset, margin - offset + length, axis=direction
        )
        contrib = weight * (upper_cells - lower_cells)
        summed = contrib if summed is None else summed + contrib
    return summed


def rates_from(padded, margin, velocity, shear_rate):
    size_x = padded.shape[1] - 2 * margin
    size_y = padded.shape[2] - 2 * margin
    interior = padded[:, margin : margin + size_x, margin : margin + size_y]
    slope_x = difference(padded[:, :, margin : margin + size_y], 1, margin, size_x)
    slope_y = difference(padded[:, margin : margin + size_x], 2, margin, size_y)
    slope_z = difference(wrap_depth(interior, 3), 3, 3, interior.shape[3])
    divergence = slope_x[1] + slope_y[2] + slope_z[3]
    return jnp.stack(
        [
            -velocity * slope_x[0] - divergence,
            -velocity * slope_x[1] - shear_rate * interior[2] - slope_x[4],
            -velocity * slope_x[2] - slope_y[4],
            -velocity * slope_x[3] - slope_z[4],
            -velocity * slope_x[4] - divergence,
        ]
    )


def adjoint_fields(adjoint_in, velocity):
    acoustic = adjoint_in[0] + adjoint_in[4]
    return jnp.stack(
        [
            velocity * adjoint_in[0],
            velocity * adjoint_in[1] + acoustic,
            velocity * adjoint_in[2],
            velocity * adjoint_in[3],
            velocity * adjoint_in[4] + adjoint_in[1],
            acoustic,
            adjoint_in[2],
            adjoint_in[3],
        ]
    )


def adjoint_from(padded, margin, adjoint_in, shear_rate):
    size_x = padded.shape[1] - 2 * margin
    size_y = padded.shape[2] - 2 * margin
    interior = padded[:, margin : margin + size_x, margin : margin + size_y]
    slope_x = difference(padded[:5, :, margin : margin + size_y], 1, margin, size_x)
    slope_y = difference(padded[5:, margin : margin + size_x], 2, margin, size_y)
    slope_z = difference(wrap_depth(interior[5:], 3), 3, 3, interior.shape[3])
    return jnp.stack(
        [
            slope_x[0],
            slope_x[1],
            slope_x[2] - shear_rate * adjoint_in[1] + slope_y[0],
            slope_x[3] + slope_z[0],
            slope_x[4] + slope_y[1] + slope_z[2],
        ]
    )


def conv_valid(padded, kernel):
    return lax.conv_general_dilated(
        padded[None],
        kernel,
        (1, 1, 1),
        "VALID",
        dimension_numbers=("NCDHW", "OIDHW", "NCDHW"),
        preferred_element_type=jnp.float32,
    )[0]


def flip_kernel(kernel):
    return jnp.transpose(jnp.flip(kernel, (2, 3, 4)), (1, 0, 2, 3, 4))


def kernel_grad(padded, gradient):
    channels = padded.shape[0]
    size_x, size_y, size_z = (gradient.shape[1], gradient.shape[2], gradient.shape[3])
    flat_grad = gradient.reshape(gradient.shape[0], -1)
    pieces = []
    for shift_x in range(3):
        for shift_y in range(3):
            for shift_z in range(3):
                window = padded[
                    :,
                    shift_x : shift_x + size_x,
                    shift_y : shift_y + size_y,
                    shift_z : shift_z + size_z,
                ]
                pieces.append(
                    lax.dot_general(
                        flat_grad,
                        window.reshape(channels, -1),
                        (((1,), (1,)), ((), ())),
                        preferred_element_type=jnp.float32,
                    )
                )
    stacked = jnp.stack(pieces)
    return jnp.transpose(stacked, (1, 2, 0)).reshape(gradient.shape[0], channels * 27)


def closure_backward(saved, source_grad, kernels, need_input, padding_fn):
    kernel_in, kernel_mid, kernel_out = kernels
    padded_in, hidden_one, padded_one, hidden_two, padded_two = saved
    error_out = source_grad.astype(jnp.bfloat16)
    grad_out = kernel_grad(padded_two, error_out)
    back_mid = conv_valid(padding_fn(error_out), flip_kernel(kernel_out)) * (
        1.0 - jnp.square(hidden_two.astype(jnp.float32))
    )
    error_mid = back_mid.astype(jnp.bfloat16)
    grad_mid = kernel_grad(padded_one, error_mid)
    back_in = conv_valid(padding_fn(error_mid), flip_kernel(kernel_mid)) * (
        1.0 - jnp.square(hidden_one.astype(jnp.float32))
    )
    error_in = back_in.astype(jnp.bfloat16)
    grad_in = kernel_grad(padded_in, error_in)
    state_grad = conv_valid(padding_fn(error_in), flip_kernel(kernel_in)) if need_input else None
    return ((grad_in, grad_mid, grad_out), state_grad)


def retreat(adjoint_in, adjoint_fn):
    into_second = 2.0 / 3.0 * adjoint_in + 2.0 / 3.0 * TIME_STEP * adjoint_fn(adjoint_in)
    direct = 1.0 / 3.0 * adjoint_in
    into_first = 0.25 * into_second + 0.25 * TIME_STEP * adjoint_fn(into_second)
    direct = direct + 0.75 * into_second
    carried = direct + into_first + TIME_STEP * adjoint_fn(into_first)
    source_grad = TIME_STEP * (2.0 / 3.0 * adjoint_in + 0.25 * into_second + into_first)
    return (carried, source_grad)


def grad_pad(grid_field):
    return wrap_depth(padded_2(grid_field, (("gx", 1), ("gy", 2)), 1), 1)


def inside(size_x, size_y, margin):
    start_x = lax.axis_index("gx") * size_x - margin
    start_y = lax.axis_index("gy") * size_y - margin
    index_x = start_x + jnp.arange(size_x + 2 * margin, dtype=jnp.int32)
    index_y = start_y + jnp.arange(size_y + 2 * margin, dtype=jnp.int32)
    valid_x = (index_x >= 0) & (index_x < size_x * lax.axis_size("gx"))
    valid_y = (index_y >= 0) & (index_y < size_y * lax.axis_size("gy"))
    return (valid_x[:, None] & valid_y[None, :]).astype(jnp.float32)[None, :, :, None]


def closure_deep(grid_field, kernels):
    kernel_in, kernel_mid, kernel_out = kernels
    size_x, size_y = (grid_field.shape[1], grid_field.shape[2])
    extended = padded_2(grid_field, (("gx", 1), ("gy", 2)), 3)
    input_wide = extended.astype(jnp.bfloat16)
    hidden_wide = (
        jnp.tanh(conv_valid(wrap_depth(input_wide, 1), kernel_in)) * inside(size_x, size_y, 2)
    ).astype(jnp.bfloat16)
    second_wide = (
        jnp.tanh(conv_valid(wrap_depth(hidden_wide, 1), kernel_mid)) * inside(size_x, size_y, 1)
    ).astype(jnp.bfloat16)
    source = conv_valid(wrap_depth(second_wide, 1), kernel_out)
    saved = (
        wrap_depth(input_wide[:, 2:-2, 2:-2], 1),
        hidden_wide[:, 2:-2, 2:-2],
        wrap_depth(hidden_wide[:, 1:-1, 1:-1], 1),
        second_wide[:, 1:-1, 1:-1],
        wrap_depth(second_wide, 1),
    )
    return (extended, source, saved)


def body(perturbation, mean_velocity, mean_shear, cotangent, kernel_in, kernel_mid, kernel_out):
    channels = perturbation.shape[0]
    hidden = kernel_in.shape[0]
    size_x = perturbation.shape[1]
    size_y = perturbation.shape[2] // NZ
    current = perturbation.reshape(channels, size_x, size_y, NZ)
    velocity = mean_velocity.reshape(size_x, size_y, NZ)
    shear_rate = mean_shear.reshape(size_x, size_y, NZ)
    kernels = (
        kernel_in.reshape(hidden, channels, 3, 3, 3),
        kernel_mid.reshape(hidden, hidden, 3, 3, 3),
        kernel_out.reshape(channels, hidden, 3, 3, 3),
    )

    def section_rates(grid_field):
        padded = padded_2(grid_field, (("gx", 1), ("gy", 2)), 3)
        return rates_from(padded, 3, velocity, shear_rate)

    def adjoint_rates(adjoint_in):
        padded = padded_2(adjoint_fields(adjoint_in, velocity), (("gx", 1), ("gy", 2)), 3)
        return adjoint_from(padded, 3, adjoint_in, shear_rate)

    def evaluate(grid_field, with_rates):
        extended, source, saved = closure_deep(grid_field, kernels)
        rate_field = rates_from(extended, 3, velocity, shear_rate) if with_rates else None
        return (source, saved, rate_field)

    history = []
    stored = []
    for step_index in range(STEPS):
        source, saved, rate_field = evaluate(current, True)
        history.append(current)
        stored.append(saved)
        section_one = current + TIME_STEP * (rate_field + source)
        section_two = 0.75 * current + 0.25 * (
            section_one + TIME_STEP * (section_rates(section_one) + source)
        )
        current = 1.0 / 3.0 * current + 2.0 / 3.0 * (
            section_two + TIME_STEP * (section_rates(section_two) + source)
        )
    cell_count = size_x * lax.axis_size("gx") * size_y * lax.axis_size("gy") * NZ
    adjoint_in = cotangent.reshape(channels, size_x, size_y, NZ) * (1.0 / math.sqrt(cell_count))
    totals = None
    for step_index in reversed(range(STEPS)):
        carried, source_grad = retreat(adjoint_in, adjoint_rates)
        saved = evaluate(history[step_index], False)[1]
        kernel_grads, state_grad = closure_backward(
            saved, source_grad, kernels, step_index > 0, grad_pad
        )
        totals = (
            kernel_grads
            if totals is None
            else tuple((sum_old + sum_new for sum_old, sum_new in zip(totals, kernel_grads)))
        )
        if step_index > 0:
            adjoint_in = carried + state_grad
    result = lax.psum((totals[0], totals[1], totals[2]), ("gx", "gy"))
    return (current.reshape(channels, size_x, size_y * NZ), result[0], result[1], result[2])


def solution(mesh):
    return jax.shard_map(
        body,
        mesh=mesh,
        in_specs=(
            P(None, "gx", "gy"),
            P("gx", "gy"),
            P("gx", "gy"),
            P(None, "gx", "gy"),
            P(),
            P(),
            P(),
        ),
        out_specs=(P(None, "gx", "gy"), P(), P(), P()),
        check_vma=False,
    )
```

profile of v0, /device:TPU:0, one launch (start us, length us, event | category | flops | bytes accessed | tf_op | source)
XLA Modules:
  0.0 642.7 jit_solution(11449475301091532205)
XLA Ops:
  14.4 5.8 collective-permute-start.25
  35.9 5.2 collective-permute-start.27
  50.0 5.2 fusion.164
  77.6 5.0 collective-permute-done.30
  92.4 7.0 %collective-permute-start.32 = (bf16[5,1,8,8]{3,2,1,0:T(8,128)(2,1)S(1)}, bf16[5,1,8,8]{3,2,1,0:T(8,128)(2,1)S(1)}, u32[]{:S(2)}, u32[]{:S(2)}) collective-permute-start(bf16[5,1,8,8]{3,2,1,0:T(8,128)(2,1)S(1)} %get-tuple-element.302), channel_id=1, source_target_pairs={{0,8},{8,16},{16,24},{1,9},{9,17},{17,25},{2,10},{10,18},{18,26},{... | collective-permute-start | bytes 1928 | tf_op jit(solution)/shard_map/ppermute | solution.py:21
  101.6 5.4 collective-permute-start.34
  120.1 4.6 collective-permute-start.43
  133.9 5.4 collective-permute-start.11
  141.6 5.2 collective-permute-done.10
  155.3 4.8 collective-permute-start.15
  174.6 5.2 fusion.162
  206.7 4.5 collective-permute-start.38
  232.7 5.0 collective-permute-start.46
  249.0 4.5 collective-permute-start.51
  256.6 5.3 collective-permute-done.50
  269.0 5.0 collective-permute-start.17
  277.2 4.8 collective-permute-start.19
  283.7 5.2 collective-permute-start.55
  291.5 5.4 collective-permute-done.54
  340.2 4.7 collective-permute-start.62
  371.5 4.9 collective-permute-start.23
  379.7 5.2 collective-permute-done.22
  386.8 111.3 %all-reduce.6.cloned.1.call-done = (f32[64,135]{0,1:T(8,128)}, f32[5,1728]{1,0:T(8,128)}) async-done(((f32[64,135]{0,1:T(8,128)}, f32[5,1728]{1,0:T(8,128)}), (f32[64,135]{0,1:T(8,128)}, f32[5,1728]{1,0:T(8,128)})) %all-reduce.6.cloned.1.call-update) | async-done | bytes 69136 | tf_op jit(solution)/shard_map/psum | solution.py:266
  499.7 133.0 %all-reduce.4.cloned.1.call-done = f32[64,1728]{0,1:T(8,128)} async-done(((f32[64,1728]{0,1:T(8,128)}), f32[64,1728]{0,1:T(8,128)}) %all-reduce.4.cloned.1.call-update) | async-done | bytes 442384 | tf_op jit(solution)/shard_map/psum | solution.py:266
  (823 shorter events, 267.3 us)
Async XLA Ops:
  7.2 491.0 %all-reduce.6.cloned.1.call-start = ((), (), s32[]{:S(2)}) async-start(), calls=%async_computation.1 | async-start | bytes 253952 | tf_op jit(solution)/shard_map/psum | solution.py:266
  8.0 21.2 %collective-permute-start.1 = (f32[5,3,8,8]{3,2,1,0:T(8,128)S(1)}, f32[5,3,8,8]{3,2,1,0:T(8,128)S(1)}, u32[]{:S(2)}, u32[]{:S(2)}) collective-permute-start(f32[5,3,8,8]{3,2,1,0:T(8,128)S(1)} %get-tuple-element.273), channel_id=1, source_target_pairs={{0,8},{8,16},{16,24},{1,9},{9,17},{17,25},{2,10},{10,18},{18,26},{... | collective-permute-start | bytes 11528 | tf_op jit(solution)/shard_map/ppermute | solution.py:21
  10.5 19.8 %collective-permute-start = (f32[5,3,8,8]{3,2,1,0:T(8,128)S(1)}, f32[5,3,8,8]{3,2,1,0:T(8,128)S(1)}, u32[]{:S(2)}, u32[]{:S(2)}) collective-permute-start(f32[5,3,8,8]{3,2,1,0:T(8,128)S(1)} %get-tuple-element.272), channel_id=1, source_target_pairs={{8,0},{16,8},{24,16},{9,1},{17,9},{25,17},{10,2},{18,10},{26,18},{... | collective-permute-start | bytes 11528 | tf_op jit(solution)/shard_map/ppermute | solution.py:23
  13.1 21.9 %collective-permute-start.24 = (f32[8,3,8,8]{3,2,1,0:T(8,128)S(1)}, f32[8,3,8,8]{3,2,1,0:T(8,128)S(1)}, u32[]{:S(2)}, u32[]{:S(2)}) collective-permute-start(f32[8,3,8,8]{3,2,1,0:T(8,128)S(1)} %get-tuple-element.202), channel_id=1, source_target_pairs={{8,0},{16,8},{24,16},{9,1},{17,9},{25,17},{10,2},{18,10},{26,18},{... | collective-permute-start | bytes 18440 | tf_op jit(solution)/shard_map/ppermute | solution.py:23
  14.4 20.6 %collective-permute-start.25 = (f32[8,3,8,8]{3,2,1,0:T(8,128)S(1)}, f32[8,3,8,8]{3,2,1,0:T(8,128)S(1)}, u32[]{:S(2)}, u32[]{:S(2)}) collective-permute-start(f32[8,3,8,8]{3,2,1,0:T(8,128)S(1)} %get-tuple-element.201), channel_id=1, source_target_pairs={{0,8},{8,16},{16,24},{1,9},{9,17},{17,25},{2,10},{10,18},{18,26},{... | collective-permute-start | bytes 18440 | tf_op jit(solution)/shard_map/ppermute | solution.py:21
  35.9 27.0 %collective-permute-start.27 = (f32[8,10,3,8]{3,2,1,0:T(4,128)}, f32[8,10,3,8]{3,2,1,0:T(4,128)}, u32[]{:S(2)}, u32[]{:S(2)}) collective-permute-start(f32[8,10,3,8]{3,2,1,0:T(4,128)} %get-tuple-element.95), channel_id=1, source_target_pairs={{0,1},{1,2},{2,3},{3,4},{4,5},{5,6},{6,7},{8,9},{9,10},{10,11},{11... | collective-permute-start | bytes 23048 | tf_op jit(solution)/shard_map/ppermute | solution.py:21
  41.1 21.8 %collective-permute-start.26 = (f32[8,10,3,8]{3,2,1,0:T(4,128)}, f32[8,10,3,8]{3,2,1,0:T(4,128)}, u32[]{:S(2)}, u32[]{:S(2)}) collective-permute-start(f32[8,10,3,8]{3,2,1,0:T(4,128)} %get-tuple-element.94), channel_id=1, source_target_pairs={{1,0},{2,1},{3,2},{4,3},{5,4},{6,5},{7,6},{9,8},{10,9},{11,10},{12... | collective-permute-start | bytes 23048 | tf_op jit(solution)/shard_map/ppermute | solution.py:23
  85.2 28.6 %collective-permute-start.5 = (f32[5,3,8,8]{3,2,1,0:T(8,128)S(1)}, f32[5,3,8,8]{3,2,1,0:T(8,128)S(1)}, u32[]{:S(2)}, u32[]{:S(2)}) collective-permute-start(f32[5,3,8,8]{3,2,1,0:T(8,128)S(1)} %get-tuple-element.264), channel_id=1, source_target_pairs={{0,8},{8,16},{16,24},{1,9},{9,17},{17,25},{2,10},{10,18},{18,26},{... | collective-permute-start | bytes 11528 | tf_op jit(solution)/shard_map/ppermute | solution.py:21
  88.4 25.4 %collective-permute-start.4 = (f32[5,3,8,8]{3,2,1,0:T(8,128)S(1)}, f32[5,3,8,8]{3,2,1,0:T(8,128)S(1)}, u32[]{:S(2)}, u32[]{:S(2)}) collective-permute-start(f32[5,3,8,8]{3,2,1,0:T(8,128)S(1)} %get-tuple-element.265), channel_id=1, source_target_pairs={{8,0},{16,8},{24,16},{9,1},{17,9},{25,17},{10,2},{18,10},{26,18},{... | collective-permute-start | bytes 11528 | tf_op jit(solution)/shard_map/ppermute | solution.py:23
  89.7 30.3 %collective-permute-start.40 = (f32[8,3,8,8]{3,2,1,0:T(8,128)S(1)}, f32[8,3,8,8]{3,2,1,0:T(8,128)S(1)}, u32[]{:S(2)}, u32[]{:S(2)}) collective-permute-start(f32[8,3,8,8]{3,2,1,0:T(8,128)S(1)} %get-tuple-element.192), channel_id=1, source_target_pairs={{8,0},{16,8},{24,16},{9,1},{17,9},{25,17},{10,2},{18,10},{26,18},{... | collective-permute-start | bytes 18440 | tf_op jit(solution)/shard_map/ppermute | solution.py:23
  120.1 20.9 %collective-permute-start.43 = (f32[8,10,3,8]{3,2,1,0:T(4,128)S(1)}, f32[8,10,3,8]{3,2,1,0:T(4,128)S(1)}, u32[]{:S(2)}, u32[]{:S(2)}) collective-permute-start(f32[8,10,3,8]{3,2,1,0:T(4,128)S(1)} %get-tuple-element.91), channel_id=1, source_target_pairs={{0,1},{1,2},{2,3},{3,4},{4,5},{5,6},{6,7},{8,9},{9,10},{10,11},{11... | collective-permute-start | bytes 23048 | tf_op jit(solution)/shard_map/ppermute | solution.py:21
  124.7 16.3 %collective-permute-start.42 = (f32[8,10,3,8]{3,2,1,0:T(4,128)S(1)}, f32[8,10,3,8]{3,2,1,0:T(4,128)S(1)}, u32[]{:S(2)}, u32[]{:S(2)}) collective-permute-start(f32[8,10,3,8]{3,2,1,0:T(4,128)S(1)} %get-tuple-element.90), channel_id=1, source_target_pairs={{1,0},{2,1},{3,2},{4,3},{5,4},{6,5},{7,6},{9,8},{10,9},{11,10},{12... | collective-permute-start | bytes 23048 | tf_op jit(solution)/shard_map/ppermute | solution.py:23
  180.0 24.7 %collective-permute-start.37 = (bf16[64,1,8,8]{0,3,2,1:T(8,128)(2,1)S(1)}, bf16[64,1,8,8]{0,3,2,1:T(8,128)(2,1)S(1)}, u32[]{:S(2)}, u32[]{:S(2)}) collective-permute-start(bf16[64,1,8,8]{0,3,2,1:T(8,128)(2,1)S(1)} %get-tuple-element.281), channel_id=1, source_target_pairs={{8,0},{16,8},{24,16},{9,1},{17,9},{25,17},{10,2},{18,10},{26,18},{... | collective-permute-start | bytes 24584 | tf_op jit(solution)/shard_map/ppermute | solution.py:23
  181.3 23.4 %collective-permute-start.36 = (bf16[64,1,8,8]{0,3,2,1:T(8,128)(2,1)S(1)}, bf16[64,1,8,8]{0,3,2,1:T(8,128)(2,1)S(1)}, u32[]{:S(2)}, u32[]{:S(2)}) collective-permute-start(bf16[64,1,8,8]{0,3,2,1:T(8,128)(2,1)S(1)} %get-tuple-element.280), channel_id=1, source_target_pairs={{0,8},{8,16},{16,24},{1,9},{9,17},{17,25},{2,10},{10,18},{18,26},{... | collective-permute-start | bytes 24584 | tf_op jit(solution)/shard_map/ppermute | solution.py:21
  214.1 17.3 %collective-permute-start.45 = (bf16[64,1,8,8]{0,3,2,1:T(8,128)(2,1)S(1)}, bf16[64,1,8,8]{0,3,2,1:T(8,128)(2,1)S(1)}, u32[]{:S(2)}, u32[]{:S(2)}) collective-permute-start(bf16[64,1,8,8]{0,3,2,1:T(8,128)(2,1)S(1)} %get-tuple-element.279), channel_id=1, source_target_pairs={{8,0},{16,8},{24,16},{9,1},{17,9},{25,17},{10,2},{18,10},{26,18},{... | collective-permute-start | bytes 24584 | tf_op jit(solution)/shard_map/ppermute | solution.py:23
  215.4 16.0 %collective-permute-start.44 = (bf16[64,1,8,8]{0,3,2,1:T(8,128)(2,1)S(1)}, bf16[64,1,8,8]{0,3,2,1:T(8,128)(2,1)S(1)}, u32[]{:S(2)}, u32[]{:S(2)}) collective-permute-start(bf16[64,1,8,8]{0,3,2,1:T(8,128)(2,1)S(1)} %get-tuple-element.278), channel_id=1, source_target_pairs={{0,8},{8,16},{16,24},{1,9},{9,17},{17,25},{2,10},{10,18},{18,26},{... | collective-permute-start | bytes 24584 | tf_op jit(solution)/shard_map/ppermute | solution.py:21
  263.9 19.7 %collective-permute-start.52 = (f32[8,3,8,8]{3,2,1,0:T(8,128)S(1)}, f32[8,3,8,8]{3,2,1,0:T(8,128)S(1)}, u32[]{:S(2)}, u32[]{:S(2)}) collective-permute-start(f32[8,3,8,8]{3,2,1,0:T(8,128)S(1)} %get-tuple-element.182), channel_id=1, source_target_pairs={{8,0},{16,8},{24,16},{9,1},{17,9},{25,17},{10,2},{18,10},{26,18},{... | collective-permute-start | bytes 18440 | tf_op jit(solution)/shard_map/ppermute | solution.py:23
  265.2 18.4 %collective-permute-start.53 = (f32[8,3,8,8]{3,2,1,0:T(8,128)S(1)}, f32[8,3,8,8]{3,2,1,0:T(8,128)S(1)}, u32[]{:S(2)}, u32[]{:S(2)}) collective-permute-start(f32[8,3,8,8]{3,2,1,0:T(8,128)S(1)} %get-tuple-element.181), channel_id=1, source_target_pairs={{0,8},{8,16},{16,24},{1,9},{9,17},{17,25},{2,10},{10,18},{18,26},{... | collective-permute-start | bytes 18440 | tf_op jit(solution)/shard_map/ppermute | solution.py:21
  277.2 13.1 %collective-permute-start.19 = (f32[5,10,3,8]{3,2,1,0:T(4,128)S(1)}, f32[5,10,3,8]{3,2,1,0:T(4,128)S(1)}, u32[]{:S(2)}, u32[]{:S(2)}) collective-permute-start(f32[5,10,3,8]{3,2,1,0:T(4,128)S(1)} %get-tuple-element.141), channel_id=1, source_target_pairs={{0,1},{1,2},{2,3},{3,4},{4,5},{5,6},{6,7},{8,9},{9,10},{10,11},{11... | collective-permute-start | bytes 14408 | tf_op jit(solution)/shard_map/ppermute | solution.py:21
  299.9 71.5 %collective-permute-start.21 = (f32[5,3,8,8]{3,2,1,0:T(8,128)}, f32[5,3,8,8]{3,2,1,0:T(8,128)S(1)}, u32[]{:S(2)}, u32[]{:S(2)}) collective-permute-start(f32[5,3,8,8]{3,2,1,0:T(8,128)} %get-tuple-element.243), channel_id=1, source_target_pairs={{0,8},{8,16},{16,24},{1,9},{9,17},{17,25},{2,10},{10,18},{18,26},{... | collective-permute-start | bytes 11528 | tf_op jit(solution)/shard_map/ppermute | solution.py:21
  302.7 68.7 %collective-permute-start.20 = (f32[5,3,8,8]{3,2,1,0:T(8,128)}, f32[5,3,8,8]{3,2,1,0:T(8,128)S(1)}, u32[]{:S(2)}, u32[]{:S(2)}) collective-permute-start(f32[5,3,8,8]{3,2,1,0:T(8,128)} %get-tuple-element.242), channel_id=1, source_target_pairs={{8,0},{16,8},{24,16},{9,1},{17,9},{25,17},{10,2},{18,10},{26,18},{... | collective-permute-start | bytes 11528 | tf_op jit(solution)/shard_map/ppermute | solution.py:23
  304.3 13.8 %collective-permute-start.57 = (bf16[5,1,8,8]{3,2,1,0:T(8,128)(2,1)S(1)}, bf16[5,1,8,8]{3,2,1,0:T(8,128)(2,1)S(1)}, u32[]{:S(2)}, u32[]{:S(2)}) collective-permute-start(bf16[5,1,8,8]{3,2,1,0:T(8,128)(2,1)S(1)} %get-tuple-element.301), channel_id=1, source_target_pairs={{8,0},{16,8},{24,16},{9,1},{17,9},{25,17},{10,2},{18,10},{26,18},{... | collective-permute-start | bytes 1928 | tf_op jit(solution)/shard_map/ppermute | solution.py:23
  305.6 12.5 %collective-permute-start.56 = (bf16[5,1,8,8]{3,2,1,0:T(8,128)(2,1)S(1)}, bf16[5,1,8,8]{3,2,1,0:T(8,128)(2,1)S(1)}, u32[]{:S(2)}, u32[]{:S(2)}) collective-permute-start(bf16[5,1,8,8]{3,2,1,0:T(8,128)(2,1)S(1)} %get-tuple-element.300), channel_id=1, source_target_pairs={{0,8},{8,16},{16,24},{1,9},{9,17},{17,25},{2,10},{10,18},{18,26},{... | collective-permute-start | bytes 1928 | tf_op jit(solution)/shard_map/ppermute | solution.py:21
  369.3 263.5 %all-reduce.4.cloned.1.call-start = ((), (), s32[]{:S(2)}) async-start(), calls=%async_computation | async-start | bytes 1769472 | tf_op jit(solution)/shard_map/psum | solution.py:266
  (148 other events, 652.0 us)
Sparse Core Ops, SparseCore 0:
  369.4 128.6 all-reduce.5
  503.3 129.3 all-reduce.3
where the time goes:
time: 652 us; the launch traced here: 643 us
  waiting for transfers between devices  289 us (44%)
  starting transfers between devices  182 us (28%)
  local copies, waits for them, and re-layouts  68.4 us (10%)
  matrix products  65.6 us (10%)
  other arithmetic  20.1 us (3%)
  between operations  17.5 us (3%)
    psum x2, waiting for transfers between devices, body(): result = lax.psum((totals[0], totals[1], totals[2]), ('gx', 'gy'))  244 us
    ppermute x32, starting transfers between devices, padded_2(): lax.ppermute(tail, axis, [(i, (i + 1) % count) for i in range(ends)])  140 us
    ppermute x32, starting transfers between devices, padded_2(): lax.ppermute(head, axis, [((i + 1) % count, i) for i in range(ends)])  41.7 us
    unnamed x240, local copies, waits for them, and re-layouts  40.9 us
    dot_general x162, matrix products, kernel_grad(): lax.dot_general(flat_grad, window.reshape(channels, -1), (((1,), (1,)), (...  37 us
    ppermute x32, waiting for transfers between devices, padded_2(): lax.ppermute(head, axis, [((i + 1) % count, i) for i in range(ends)])  35.6 us
    conv_general_dilated x11, matrix products, conv_valid(): lax.conv_general_dilated(padded[None], kernel, (1, 1, 1), 'VALID', dimens...  28.6 us
  transfers between devices with their start and end apart: 66, of which 22 were waited for; matrix products, arithmetic and copies ran while one was open for 14% of the time, Pallas kernels for 0%

commit v1 on v0

--- a/solution.py
+++ b/solution.py
@@ -263,7 +263,9 @@
         )
         if step_index > 0:
             adjoint_in = carried + state_grad
-    result = lax.psum((totals[0], totals[1], totals[2]), ("gx", "gy"))
+    result = (totals[0], totals[1], totals[2])
+    for b in ("gy", "gx"):
+        result = lax.psum(result, b)
     return (current.reshape(channels, size_x, size_y * NZ), result[0], result[1], result[2])
 
 

time: 652 us -> 614 us (0.942)
  waiting for transfers between devices: 289 us -> 252 us
    psum x2 -> x4, waiting for transfers between devices: 244 us -> 206 us  [body(): result = lax.psum(result, b)]
  transfers between devices with their start and end apart: 66 -> 68, of which waited for: 22 -> 24; matrix products, arithmetic and copies ran while one was open for 14% -> 15% of each run, Pallas kernels for 0% -> 0%
where the time goes in v1:
time: 614 us; the launch traced here: 605 us
  waiting for transfers between devices  252 us (41%)
  starting transfers between devices  182 us (30%)
  local copies, waits for them, and re-layouts  68.5 us (11%)
  matrix products  65.6 us (11%)
  other arithmetic  20.1 us (3%)
  between operations  17.2 us (3%)
    psum x4, waiting for transfers between devices, body(): result = lax.psum(result, b)  206 us
    ppermute x32, starting transfers between devices, padded_2(): lax.ppermute(tail, axis, [(i, (i + 1) % count) for i in range(ends)])  140 us
    ppermute x32, starting transfers between devices, padded_2(): lax.ppermute(head, axis, [((i + 1) % count, i) for i in range(ends)])  41.7 us
    unnamed x240, local copies, waits for them, and re-layouts  41 us
    dot_general x162, matrix products, kernel_grad(): lax.dot_general(flat_grad, window.reshape(channels, -1), (((1,), (1,)), (...  37 us
    ppermute x32, waiting for transfers between devices, padded_2(): lax.ppermute(head, axis, [((i + 1) % count, i) for i in range(ends)])  35.2 us
    conv_general_dilated x11, matrix products, conv_valid(): lax.conv_general_dilated(padded[None], kernel, (1, 1, 1), 'VALID', dimens...  28.6 us
  transfers between devices with their start and end apart: 68, of which 24 were waited for; matrix products, arithmetic and copies ran while one was open for 15% of the time, Pallas kernels for 0%

profile of v1, /device:TPU:0, one launch (start us, length us, event | category | flops | bytes accessed | tf_op | source)
XLA Modules:
  0.0 604.7 jit_solution(5786832606067728861)
XLA Ops:
  14.4 5.8 collective-permute-start.25
  35.9 5.2 collective-permute-start.27
  49.9 5.2 fusion.164
  77.6 5.0 collective-permute-done.30
  92.4 7.0 %collective-permute-start.32 = (bf16[5,1,8,8]{3,2,1,0:T(8,128)(2,1)S(1)}, bf16[5,1,8,8]{3,2,1,0:T(8,128)(2,1)S(1)}, u32[]{:S(2)}, u32[]{:S(2)}) collective-permute-start(bf16[5,1,8,8]{3,2,1,0:T(8,128)(2,1)S(1)} %get-tuple-element.304), channel_id=1, source_target_pairs={{0,8},{8,16},{16,24},{1,9},{9,17},{17,25},{2,10},{10,18},{18,26},{... | collective-permute-start | bytes 1928 | tf_op jit(solution)/shard_map/ppermute | solution.py:21
  101.6 5.4 collective-permute-start.34
  120.1 4.6 collective-permute-start.43
  133.9 5.4 collective-permute-start.11
  141.6 5.2 collective-permute-done.10
  155.3 4.8 collective-permute-start.15
  174.6 5.2 fusion.162
  232.7 5.0 collective-permute-start.46
  256.6 5.3 collective-permute-done.50
  269.0 5.0 collective-permute-start.17
  277.1 4.8 collective-permute-start.19
  283.7 5.2 collective-permute-start.55
  291.5 5.4 collective-permute-done.54
  340.2 4.7 collective-permute-start.62
  371.6 4.9 collective-permute-start.23
  380.0 4.9 collective-permute-done.22
  385.5 58.9 %all-reduce.11.cloned.1.call-done = (f32[64,135]{0,1:T(8,128)}, f32[5,1728]{1,0:T(8,128)}) async-done(((f32[64,135]{0,1:T(8,128)}, f32[5,1728]{1,0:T(8,128)}), (f32[64,135]{0,1:T(8,128)}, f32[5,1728]{1,0:T(8,128)})) %all-reduce.11.cloned.1.call-update) | async-done | bytes 69136 | tf_op jit(solution)/shard_map/psum | solution.py:268
  444.5 79.3 %all-reduce.7.cloned.1.call-done = f32[64,1728]{0,1:T(8,128)} async-done(((f32[64,1728]{0,1:T(8,128)}), f32[64,1728]{0,1:T(8,128)}) %all-reduce.7.cloned.1.call-update) | async-done | bytes 442384 | tf_op jit(solution)/shard_map/psum | solution.py:268
  525.3 31.9 %all-reduce.13.cloned.1.call-done = (f32[64,135]{0,1:T(8,128)}, f32[5,1728]{1,0:T(8,128)}) async-done(((f32[64,135]{0,1:T(8,128)}, f32[5,1728]{1,0:T(8,128)}), (f32[64,135]{0,1:T(8,128)}, f32[5,1728]{1,0:T(8,128)})) %all-reduce.13.cloned.1.call-update) | async-done | bytes 69136 | tf_op jit(solution)/shard_map/psum | solution.py:268
  558.7 36.3 %all-reduce.9.cloned.1.call-done = f32[64,1728]{0,1:T(8,128)} async-done(((f32[64,1728]{0,1:T(8,128)}), f32[64,1728]{0,1:T(8,128)}) %all-reduce.9.cloned.1.call-update) | async-done | bytes 442384 | tf_op jit(solution)/shard_map/psum | solution.py:268
  (829 shorter events, 276.8 us)
Async XLA Ops:
  7.2 437.3 %all-reduce.11.cloned.1.call-start = ((), (), s32[]{:S(2)}) async-start(), calls=%async_computation.2 | async-start | bytes 253952 | tf_op jit(solution)/shard_map/psum | solution.py:268
  8.0 21.2 %collective-permute-start.1 = (f32[5,3,8,8]{3,2,1,0:T(8,128)S(1)}, f32[5,3,8,8]{3,2,1,0:T(8,128)S(1)}, u32[]{:S(2)}, u32[]{:S(2)}) collective-permute-start(f32[5,3,8,8]{3,2,1,0:T(8,128)S(1)} %get-tuple-element.275), channel_id=1, source_target_pairs={{0,8},{8,16},{16,24},{1,9},{9,17},{17,25},{2,10},{10,18},{18,26},{... | collective-permute-start | bytes 11528 | tf_op jit(solution)/shard_map/ppermute | solution.py:21
  10.5 19.8 %collective-permute-start = (f32[5,3,8,8]{3,2,1,0:T(8,128)S(1)}, f32[5,3,8,8]{3,2,1,0:T(8,128)S(1)}, u32[]{:S(2)}, u32[]{:S(2)}) collective-permute-start(f32[5,3,8,8]{3,2,1,0:T(8,128)S(1)} %get-tuple-element.274), channel_id=1, source_target_pairs={{8,0},{16,8},{24,16},{9,1},{17,9},{25,17},{10,2},{18,10},{26,18},{... | collective-permute-start | bytes 11528 | tf_op jit(solution)/shard_map/ppermute | solution.py:23
  13.1 21.9 %collective-permute-start.24 = (f32[8,3,8,8]{3,2,1,0:T(8,128)S(1)}, f32[8,3,8,8]{3,2,1,0:T(8,128)S(1)}, u32[]{:S(2)}, u32[]{:S(2)}) collective-permute-start(f32[8,3,8,8]{3,2,1,0:T(8,128)S(1)} %get-tuple-element.204), channel_id=1, source_target_pairs={{8,0},{16,8},{24,16},{9,1},{17,9},{25,17},{10,2},{18,10},{26,18},{... | collective-permute-start | bytes 18440 | tf_op jit(solution)/shard_map/ppermute | solution.py:23
  14.4 20.6 %collective-permute-start.25 = (f32[8,3,8,8]{3,2,1,0:T(8,128)S(1)}, f32[8,3,8,8]{3,2,1,0:T(8,128)S(1)}, u32[]{:S(2)}, u32[]{:S(2)}) collective-permute-start(f32[8,3,8,8]{3,2,1,0:T(8,128)S(1)} %get-tuple-element.203), channel_id=1, source_target_pairs={{0,8},{8,16},{16,24},{1,9},{9,17},{17,25},{2,10},{10,18},{18,26},{... | collective-permute-start | bytes 18440 | tf_op jit(solution)/shard_map/ppermute | solution.py:21
  35.9 27.0 %collective-permute-start.27 = (f32[8,10,3,8]{3,2,1,0:T(4,128)}, f32[8,10,3,8]{3,2,1,0:T(4,128)}, u32[]{:S(2)}, u32[]{:S(2)}) collective-permute-start(f32[8,10,3,8]{3,2,1,0:T(4,128)} %get-tuple-element.97), channel_id=1, source_target_pairs={{0,1},{1,2},{2,3},{3,4},{4,5},{5,6},{6,7},{8,9},{9,10},{10,11},{11... | collective-permute-start | bytes 23048 | tf_op jit(solution)/shard_map/ppermute | solution.py:21
  41.1 21.8 %collective-permute-start.26 = (f32[8,10,3,8]{3,2,1,0:T(4,128)}, f32[8,10,3,8]{3,2,1,0:T(4,128)}, u32[]{:S(2)}, u32[]{:S(2)}) collective-permute-start(f32[8,10,3,8]{3,2,1,0:T(4,128)} %get-tuple-element.96), channel_id=1, source_target_pairs={{1,0},{2,1},{3,2},{4,3},{5,4},{6,5},{7,6},{9,8},{10,9},{11,10},{12... | collective-permute-start | bytes 23048 | tf_op jit(solution)/shard_map/ppermute | solution.py:23
  85.1 28.6 %collective-permute-start.5 = (f32[5,3,8,8]{3,2,1,0:T(8,128)S(1)}, f32[5,3,8,8]{3,2,1,0:T(8,128)S(1)}, u32[]{:S(2)}, u32[]{:S(2)}) collective-permute-start(f32[5,3,8,8]{3,2,1,0:T(8,128)S(1)} %get-tuple-element.266), channel_id=1, source_target_pairs={{0,8},{8,16},{16,24},{1,9},{9,17},{17,25},{2,10},{10,18},{18,26},{... | collective-permute-start | bytes 11528 | tf_op jit(solution)/shard_map/ppermute | solution.py:21
  88.4 25.4 %collective-permute-start.4 = (f32[5,3,8,8]{3,2,1,0:T(8,128)S(1)}, f32[5,3,8,8]{3,2,1,0:T(8,128)S(1)}, u32[]{:S(2)}, u32[]{:S(2)}) collective-permute-start(f32[5,3,8,8]{3,2,1,0:T(8,128)S(1)} %get-tuple-element.267), channel_id=1, source_target_pairs={{8,0},{16,8},{24,16},{9,1},{17,9},{25,17},{10,2},{18,10},{26,18},{... | collective-permute-start | bytes 11528 | tf_op jit(solution)/shard_map/ppermute | solution.py:23
  89.7 30.3 %collective-permute-start.40 = (f32[8,3,8,8]{3,2,1,0:T(8,128)S(1)}, f32[8,3,8,8]{3,2,1,0:T(8,128)S(1)}, u32[]{:S(2)}, u32[]{:S(2)}) collective-permute-start(f32[8,3,8,8]{3,2,1,0:T(8,128)S(1)} %get-tuple-element.194), channel_id=1, source_target_pairs={{8,0},{16,8},{24,16},{9,1},{17,9},{25,17},{10,2},{18,10},{26,18},{... | collective-permute-start | bytes 18440 | tf_op jit(solution)/shard_map/ppermute | solution.py:23
  120.1 20.9 %collective-permute-start.43 = (f32[8,10,3,8]{3,2,1,0:T(4,128)S(1)}, f32[8,10,3,8]{3,2,1,0:T(4,128)S(1)}, u32[]{:S(2)}, u32[]{:S(2)}) collective-permute-start(f32[8,10,3,8]{3,2,1,0:T(4,128)S(1)} %get-tuple-element.93), channel_id=1, source_target_pairs={{0,1},{1,2},{2,3},{3,4},{4,5},{5,6},{6,7},{8,9},{9,10},{10,11},{11... | collective-permute-start | bytes 23048 | tf_op jit(solution)/shard_map/ppermute | solution.py:21
  124.7 16.3 %collective-permute-start.42 = (f32[8,10,3,8]{3,2,1,0:T(4,128)S(1)}, f32[8,10,3,8]{3,2,1,0:T(4,128)S(1)}, u32[]{:S(2)}, u32[]{:S(2)}) collective-permute-start(f32[8,10,3,8]{3,2,1,0:T(4,128)S(1)} %get-tuple-element.92), channel_id=1, source_target_pairs={{1,0},{2,1},{3,2},{4,3},{5,4},{6,5},{7,6},{9,8},{10,9},{11,10},{12... | collective-permute-start | bytes 23048 | tf_op jit(solution)/shard_map/ppermute | solution.py:23
  180.0 24.7 %collective-permute-start.37 = (bf16[64,1,8,8]{0,3,2,1:T(8,128)(2,1)S(1)}, bf16[64,1,8,8]{0,3,2,1:T(8,128)(2,1)S(1)}, u32[]{:S(2)}, u32[]{:S(2)}) collective-permute-start(bf16[64,1,8,8]{0,3,2,1:T(8,128)(2,1)S(1)} %get-tuple-element.283), channel_id=1, source_target_pairs={{8,0},{16,8},{24,16},{9,1},{17,9},{25,17},{10,2},{18,10},{26,18},{... | collective-permute-start | bytes 24584 | tf_op jit(solution)/shard_map/ppermute | solution.py:23
  181.3 23.4 %collective-permute-start.36 = (bf16[64,1,8,8]{0,3,2,1:T(8,128)(2,1)S(1)}, bf16[64,1,8,8]{0,3,2,1:T(8,128)(2,1)S(1)}, u32[]{:S(2)}, u32[]{:S(2)}) collective-permute-start(bf16[64,1,8,8]{0,3,2,1:T(8,128)(2,1)S(1)} %get-tuple-element.282), channel_id=1, source_target_pairs={{0,8},{8,16},{16,24},{1,9},{9,17},{17,25},{2,10},{10,18},{18,26},{... | collective-permute-start | bytes 24584 | tf_op jit(solution)/shard_map/ppermute | solution.py:21
  214.1 17.3 %collective-permute-start.45 = (bf16[64,1,8,8]{0,3,2,1:T(8,128)(2,1)S(1)}, bf16[64,1,8,8]{0,3,2,1:T(8,128)(2,1)S(1)}, u32[]{:S(2)}, u32[]{:S(2)}) collective-permute-start(bf16[64,1,8,8]{0,3,2,1:T(8,128)(2,1)S(1)} %get-tuple-element.281), channel_id=1, source_target_pairs={{8,0},{16,8},{24,16},{9,1},{17,9},{25,17},{10,2},{18,10},{26,18},{... | collective-permute-start | bytes 24584 | tf_op jit(solution)/shard_map/ppermute | solution.py:23
  215.4 16.0 %collective-permute-start.44 = (bf16[64,1,8,8]{0,3,2,1:T(8,128)(2,1)S(1)}, bf16[64,1,8,8]{0,3,2,1:T(8,128)(2,1)S(1)}, u32[]{:S(2)}, u32[]{:S(2)}) collective-permute-start(bf16[64,1,8,8]{0,3,2,1:T(8,128)(2,1)S(1)} %get-tuple-element.280), channel_id=1, source_target_pairs={{0,8},{8,16},{16,24},{1,9},{9,17},{17,25},{2,10},{10,18},{18,26},{... | collective-permute-start | bytes 24584 | tf_op jit(solution)/shard_map/ppermute | solution.py:21
  263.9 19.7 %collective-permute-start.52 = (f32[8,3,8,8]{3,2,1,0:T(8,128)S(1)}, f32[8,3,8,8]{3,2,1,0:T(8,128)S(1)}, u32[]{:S(2)}, u32[]{:S(2)}) collective-permute-start(f32[8,3,8,8]{3,2,1,0:T(8,128)S(1)} %get-tuple-element.184), channel_id=1, source_target_pairs={{8,0},{16,8},{24,16},{9,1},{17,9},{25,17},{10,2},{18,10},{26,18},{... | collective-permute-start | bytes 18440 | tf_op jit(solution)/shard_map/ppermute | solution.py:23
  265.2 18.4 %collective-permute-start.53 = (f32[8,3,8,8]{3,2,1,0:T(8,128)S(1)}, f32[8,3,8,8]{3,2,1,0:T(8,128)S(1)}, u32[]{:S(2)}, u32[]{:S(2)}) collective-permute-start(f32[8,3,8,8]{3,2,1,0:T(8,128)S(1)} %get-tuple-element.183), channel_id=1, source_target_pairs={{0,8},{8,16},{16,24},{1,9},{9,17},{17,25},{2,10},{10,18},{18,26},{... | collective-permute-start | bytes 18440 | tf_op jit(solution)/shard_map/ppermute | solution.py:21
  299.9 71.6 %collective-permute-start.21 = (f32[5,3,8,8]{3,2,1,0:T(8,128)}, f32[5,3,8,8]{3,2,1,0:T(8,128)S(1)}, u32[]{:S(2)}, u32[]{:S(2)}) collective-permute-start(f32[5,3,8,8]{3,2,1,0:T(8,128)} %get-tuple-element.245), channel_id=1, source_target_pairs={{0,8},{8,16},{16,24},{1,9},{9,17},{17,25},{2,10},{10,18},{18,26},{... | collective-permute-start | bytes 11528 | tf_op jit(solution)/shard_map/ppermute | solution.py:21
  302.7 68.8 %collective-permute-start.20 = (f32[5,3,8,8]{3,2,1,0:T(8,128)}, f32[5,3,8,8]{3,2,1,0:T(8,128)S(1)}, u32[]{:S(2)}, u32[]{:S(2)}) collective-permute-start(f32[5,3,8,8]{3,2,1,0:T(8,128)} %get-tuple-element.244), channel_id=1, source_target_pairs={{8,0},{16,8},{24,16},{9,1},{17,9},{25,17},{10,2},{18,10},{26,18},{... | collective-permute-start | bytes 11528 | tf_op jit(solution)/shard_map/ppermute | solution.py:23
  304.3 13.8 %collective-permute-start.57 = (bf16[5,1,8,8]{3,2,1,0:T(8,128)(2,1)S(1)}, bf16[5,1,8,8]{3,2,1,0:T(8,128)(2,1)S(1)}, u32[]{:S(2)}, u32[]{:S(2)}) collective-permute-start(bf16[5,1,8,8]{3,2,1,0:T(8,128)(2,1)S(1)} %get-tuple-element.303), channel_id=1, source_target_pairs={{8,0},{16,8},{24,16},{9,1},{17,9},{25,17},{10,2},{18,10},{26,18},{... | collective-permute-start | bytes 1928 | tf_op jit(solution)/shard_map/ppermute | solution.py:23
  369.3 154.6 %all-reduce.7.cloned.1.call-start = ((), (), s32[]{:S(2)}) async-start(), calls=%async_computation | async-start | bytes 1769472 | tf_op jit(solution)/shard_map/psum | solution.py:268
  371.4 185.7 %all-reduce.13.cloned.1.call-start = ((), (), s32[]{:S(2)}) async-start(), calls=%async_computation.3 | async-start | bytes 253952 | tf_op jit(solution)/shard_map/psum | solution.py:268
  444.5 150.6 %all-reduce.9.cloned.1.call-start = ((), (), s32[]{:S(2)}) async-start(), calls=%async_computation.1 | async-start | bytes 1769472 | tf_op jit(solution)/shard_map/psum | solution.py:268
  (150 other events, 554.7 us)
Sparse Core Ops, SparseCore 0:
  369.4 75.0 all-reduce.10
  447.9 75.9 all-reduce.6
  526.2 30.8 all-reduce.12
  559.4 35.6 all-reduce.8
